TPU v7x, 32 devices: a whole 2x2x4 slice. The times are simulated.
32 devices in a mesh: row: 4 (over x, core), col: 8 (over z, y).
Axes of the slice: x: 2, y: 2, z: 4, core: 2. Of those that a mesh axis runs over, the one named last changes fastest.
Arguments:
- vectors: float32 [8, 4096], P(None, ('row', 'col')), may hold values from -6 to 6
- diagonal: float32 [4096], P(('row', 'col'))
- blocks: float32 [4, 8, 8, 128, 128], P('row', 'col'), may hold values from -0.125 to 0.125
- block_rows: int32 [4, 8, 8], P('row', 'col'), may hold values from 0 to 7
- block_cols: int32 [4, 8, 8], P('row', 'col'), may hold values from 0 to 3
- counts: int32 [4, 8], P('row', 'col'), may hold values from 4 to 8, as said below
Outputs:
- eigvecs: float32 [8, 4096], P(None, ('row', 'col'))
- factor: float32 [8, 8], replicated
Inputs may be any that keep to these rules, and one draw needn't show every extreme that they name: `counts`: every device has at least half of its 8 slots live, and some device has all 8 live.
All inputs are finite; a program needn't handle non-finite values.
Results may differ from a plain program's by a relative error of at most 0.0001.
Values sent between devices are 32-bit elements; how exact they have to be, the bound alone decides.
No kernel may reach another device: no remote copies, remote signals or barrier semaphores. Data moves between devices by JAX's collectives and lax.ppermute only.
A program may use at most 64 MiB of HBM per device.

v0:
```python
import jax
import jax.numpy as jnp
from jax import lax
from jax.sharding import PartitionSpec as P

ITERS = 4


def solve_lower(lower, values):
    return lax.linalg.triangular_solve(lower, values, left_side=True, lower=True)


def apply_tile(tile, rows_local, cols_local, live, current, col_vectors, row_vectors):
    high = lax.Precision.HIGHEST
    nvec = current.shape[0]
    width = tile.shape[-1]
    col_count = col_vectors.shape[1] // width
    row_count = row_vectors.shape[1] // width
    slots = jnp.arange(rows_local.shape[0])
    mask = (slots < live).astype(jnp.float32)
    row_select = (rows_local[:, None] == jnp.arange(row_count)[None, :]).astype(jnp.float32) * mask[
        :, None
    ]
    col_select = (cols_local[:, None] == jnp.arange(col_count)[None, :]).astype(jnp.float32) * mask[
        :, None
    ]
    col_input = jnp.einsum(
        "bq,kqj->kbj", col_select, col_vectors.reshape(nvec, col_count, width), precision=high
    )
    direct = jnp.einsum("bij,kbj->kbi", tile, col_input, precision=high)
    direct_part = jnp.einsum("bq,kbi->kqi", row_select, direct, precision=high).reshape(
        nvec, row_count * width
    )
    row_input = jnp.einsum(
        "bq,kqi->kbi", row_select, row_vectors.reshape(nvec, row_count, width), precision=high
    )
    transposed = jnp.einsum("bij,kbi->kbj", tile, row_input, precision=high)
    transposed_part = jnp.einsum("bq,kbj->kqj", col_select, transposed, precision=high).reshape(
        nvec, col_count * width
    )
    direct_sum = lax.psum_scatter(direct_part, "col", scatter_dimension=1, tiled=True)
    transposed_sum = lax.psum_scatter(transposed_part, "row", scatter_dimension=1, tiled=True)
    return (direct_sum, transposed_sum)


def gram_factor(images):
    local_gram = jnp.dot(
        images, images.T, precision=lax.Precision.HIGHEST, preferred_element_type=jnp.float32
    )
    gram = lax.psum(local_gram, ("row", "col"))
    return jnp.linalg.cholesky(gram)


def shards(vectors, diagonal, blocks, block_rows, block_cols, counts):
    tile = blocks[0, 0]
    rows_local = block_rows[0, 0]
    cols_local = block_cols[0, 0]
    live = counts[0, 0]
    nvec = vectors.shape[0]
    current = vectors
    lower = jnp.eye(nvec, dtype=jnp.float32)
    for step in range(ITERS):
        col_vectors = lax.all_gather(current, "row", axis=1, tiled=True)
        row_vectors = lax.all_gather(current, "col", axis=1, tiled=True)
        direct_sum, transposed_sum = apply_tile(
            tile, rows_local, cols_local, live, current, col_vectors, row_vectors
        )
        images = diagonal[None, :] * current + direct_sum + transposed_sum
        lower = gram_factor(images)
        current = solve_lower(lower, images)
    return (current, lower)


def solution(mesh):
    placed = (
        P(None, ("row", "col")),
        P(("row", "col")),
        P("row", "col", None, None, None),
        P("row", "col", None),
        P("row", "col", None),
        P("row", "col"),
    )
    return jax.shard_map(
        shards,
        mesh=mesh,
        in_specs=placed,
        out_specs=(P(None, ("row", "col")), P()),
        check_vma=False,
    )
```

profile of v0, /device:TPU:0, one launch (start us, length us, event | category | flops | bytes accessed | tf_op | source)
XLA Modules:
  0.0 656.2 jit_solution(13595704017735790086)
XLA Ops:
  7.9 32.4 %all_gather.25 = f32[8,1024]{1,0:T(8,128)S(1)} all-gather(f32[8,128]{1,0:T(8,128)S(1)} %copy-done.1), channel_id=1, replica_groups=mesh['row'=4,'col'=8] {'col'}, dimensions={1}, use_global_device_ids=true | all-gather | bytes 36864 | tf_op jit(solution)/shard_map/all_gather | solution.py:64
  43.3 5.2 all_gather.24
  50.5 13.4 %reduce-scatter.11.cloned.1.call-done = f32[8,128]{1,0:T(8,128)} async-done(((f32[8,512]{1,0:T(8,128)}), f32[8,128]{1,0:T(8,128)}) %reduce-scatter.11.cloned.1.call-update) | async-done | bytes 4112 | tf_op jit(solution)/shard_map/reduce_scatter | solution.py:42
  63.9 57.9 %reduce-scatter.9.cloned.1.call-done = f32[8,128]{1,0:T(8,128)} async-done(((f32[8,1024]{1,0:T(8,128)}), f32[8,128]{1,0:T(8,128)}) %reduce-scatter.9.cloned.1.call-update) | async-done | bytes 4112 | tf_op jit(solution)/shard_map/reduce_scatter | solution.py:41
  122.6 40.1 %psum.28 = f32[8,8]{0,1:T(8,128)S(1)} all-reduce(f32[8,8]{0,1:T(8,128)S(1)} %fusion.165), channel_id=1, replica_groups=mesh['row'=4,'col'=8] {'row','col'}, use_global_device_ids=true, to_apply=%region_2.0 | all-reduce | flops 64 | bytes 512 | tf_op jit(solution)/shard_map/psum | solution.py:50
  165.7 5.5 all_gather.26
  171.2 30.6 %all_gather.27 = f32[8,1024]{1,0:T(8,128)S(1)} all-gather(f32[8,128]{1,0:T(8,128)S(1)} %fusion.55), channel_id=1, replica_groups=mesh['row'=4,'col'=8] {'col'}, dimensions={1}, use_global_device_ids=true | all-gather | bytes 36864 | tf_op jit(solution)/shard_map/all_gather | solution.py:64
  203.9 1.0 convolution_bitcast_fusion.2
  207.3 17.4 %reduce-scatter.15.cloned.1.call-done = f32[8,128]{1,0:T(8,128)} async-done(((f32[8,512]{1,0:T(8,128)}), f32[8,128]{1,0:T(8,128)}) %reduce-scatter.15.cloned.1.call-update) | async-done | bytes 4112 | tf_op jit(solution)/shard_map/reduce_scatter | solution.py:42
  224.7 57.8 %reduce-scatter.13.cloned.1.call-done = f32[8,128]{1,0:T(8,128)} async-done(((f32[8,1024]{1,0:T(8,128)}), f32[8,128]{1,0:T(8,128)}) %reduce-scatter.13.cloned.1.call-update) | async-done | bytes 4112 | tf_op jit(solution)/shard_map/reduce_scatter | solution.py:41
  283.3 40.1 %psum.29 = f32[8,8]{0,1:T(8,128)S(1)} all-reduce(f32[8,8]{0,1:T(8,128)S(1)} %fusion.166), channel_id=1, replica_groups=mesh['row'=4,'col'=8] {'row','col'}, use_global_device_ids=true, to_apply=%region_7.10 | all-reduce | flops 64 | bytes 512 | tf_op jit(solution)/shard_map/psum | solution.py:50
  326.4 5.5 all_gather.28
  331.9 30.6 %all_gather.29 = f32[8,1024]{1,0:T(8,128)S(1)} all-gather(f32[8,128]{1,0:T(8,128)S(1)} %fusion.53), channel_id=1, replica_groups=mesh['row'=4,'col'=8] {'col'}, dimensions={1}, use_global_device_ids=true | all-gather | bytes 36864 | tf_op jit(solution)/shard_map/all_gather | solution.py:64
  364.6 1.0 convolution_bitcast_fusion.1
  368.0 17.4 %reduce-scatter.19.cloned.1.call-done = f32[8,128]{1,0:T(8,128)} async-done(((f32[8,512]{1,0:T(8,128)}), f32[8,128]{1,0:T(8,128)}) %reduce-scatter.19.cloned.1.call-update) | async-done | bytes 4112 | tf_op jit(solution)/shard_map/reduce_scatter | solution.py:42
  385.4 57.8 %reduce-scatter.17.cloned.1.call-done = f32[8,128]{1,0:T(8,128)} async-done(((f32[8,1024]{1,0:T(8,128)}), f32[8,128]{1,0:T(8,128)}) %reduce-scatter.17.cloned.1.call-update) | async-done | bytes 4112 | tf_op jit(solution)/shard_map/reduce_scatter | solution.py:41
  444.1 40.3 %psum.30 = f32[8,8]{0,1:T(8,128)S(1)} all-reduce(f32[8,8]{0,1:T(8,128)S(1)} %fusion.167), channel_id=1, replica_groups=mesh['row'=4,'col'=8] {'row','col'}, use_global_device_ids=true, to_apply=%region_10.13 | all-reduce | flops 64 | bytes 512 | tf_op jit(solution)/shard_map/psum | solution.py:50
  487.3 5.5 all_gather.30
  492.8 30.6 %all_gather.31 = f32[8,1024]{1,0:T(8,128)S(1)} all-gather(f32[8,128]{1,0:T(8,128)S(1)} %fusion.51), channel_id=1, replica_groups=mesh['row'=4,'col'=8] {'col'}, dimensions={1}, use_global_device_ids=true | all-gather | bytes 36864 | tf_op jit(solution)/shard_map/all_gather | solution.py:64
  525.5 1.0 convolution_bitcast_fusion
  528.9 17.5 %reduce-scatter.23.cloned.1.call-done = f32[8,128]{1,0:T(8,128)} async-done(((f32[8,512]{1,0:T(8,128)}), f32[8,128]{1,0:T(8,128)}) %reduce-scatter.23.cloned.1.call-update) | async-done | bytes 4112 | tf_op jit(solution)/shard_map/reduce_scatter | solution.py:42
  546.4 57.9 %reduce-scatter.21.cloned.1.call-done = f32[8,128]{1,0:T(8,128)} async-done(((f32[8,1024]{1,0:T(8,128)}), f32[8,128]{1,0:T(8,128)}) %reduce-scatter.21.cloned.1.call-update) | async-done | bytes 4112 | tf_op jit(solution)/shard_map/reduce_scatter | solution.py:41
  605.1 40.1 %psum.31 = f32[8,8]{0,1:T(8,128)S(1)} all-reduce(f32[8,8]{0,1:T(8,128)S(1)} %fusion.168), channel_id=1, replica_groups=mesh['row'=4,'col'=8] {'row','col'}, use_global_device_ids=true, to_apply=%region_13.16 | all-reduce | flops 64 | bytes 512 | tf_op jit(solution)/shard_map/psum | solution.py:50
  646.7 1.2 select_bitcast_fusion
  (101 shorter events, 33.2 us)
Async XLA Ops:
  7.2 34.1 %copy-start = (f32[1,1,8,128,128]{4,3,2,1,0:T(8,128)S(1)}, f32[1,1,8,128,128]{4,3,2,1,0:T(8,128)}, u32[]{:S(2)}) copy-start(f32[1,1,8,128,128]{4,3,2,1,0:T(8,128)} %param.11) | copy-start | bytes 1572868
  7.2 0.8 copy-start.1
  7.2 56.7 %reduce-scatter.11.cloned.1.call-start = ((), (), s32[]{:S(2)}) async-start(), calls=%async_computation.9 | async-start | bytes 20480 | tf_op jit(solution)/shard_map/reduce_scatter | solution.py:42
  40.4 0.7 copy-start.3
  41.8 0.7 copy-start.2
  43.2 78.5 %reduce-scatter.9.cloned.1.call-start = ((), (), s32[]{:S(2)}) async-start(), calls=%async_computation.8 | async-start | bytes 36864 | tf_op jit(solution)/shard_map/reduce_scatter | solution.py:41
  50.5 71.3 %copy-start.4 = (f32[128]{0:T(128)S(1)}, f32[128]{0:T(128)}, u32[]{:S(2)}) copy-start(f32[128]{0:T(128)} %param.10) | copy-start | bytes 1540
  50.5 174.3 %reduce-scatter.15.cloned.1.call-start = ((), (), s32[]{:S(2)}) async-start(), calls=%async_computation.11 | async-start | bytes 20480 | tf_op jit(solution)/shard_map/reduce_scatter | solution.py:42
  206.4 76.0 %reduce-scatter.13.cloned.1.call-start = ((), (), s32[]{:S(2)}) async-start(), calls=%async_computation.10 | async-start | bytes 36864 | tf_op jit(solution)/shard_map/reduce_scatter | solution.py:41
  207.3 178.1 %reduce-scatter.19.cloned.1.call-start = ((), (), s32[]{:S(2)}) async-start(), calls=%async_computation.13 | async-start | bytes 20480 | tf_op jit(solution)/shard_map/reduce_scatter | solution.py:42
  367.1 76.1 %reduce-scatter.17.cloned.1.call-start = ((), (), s32[]{:S(2)}) async-start(), calls=%async_computation.12 | async-start | bytes 36864 | tf_op jit(solution)/shard_map/reduce_scatter | solution.py:41
  368.0 178.4 %reduce-scatter.23.cloned.1.call-start = ((), (), s32[]{:S(2)}) async-start(), calls=%async_computation.15 | async-start | bytes 20480 | tf_op jit(solution)/shard_map/reduce_scatter | solution.py:42
  528.0 76.2 %reduce-scatter.21.cloned.1.call-start = ((), (), s32[]{:S(2)}) async-start(), calls=%async_computation.14 | async-start | bytes 36864 | tf_op jit(solution)/shard_map/reduce_scatter | solution.py:41
Sparse Core Ops, SparseCore 0:
  43.4 20.4 reduce-scatter.10
  67.0 54.6 reduce-scatter.8
  206.6 18.1 reduce-scatter.14
  227.7 54.7 reduce-scatter.12
  367.3 18.1 reduce-scatter.18
  388.4 54.7 reduce-scatter.16
  528.2 18.1 reduce-scatter.22
  549.5 54.7 reduce-scatter.20
where the time goes:
time: 657 us; the launch traced here: 656 us
  blocking collectives  307 us (47%)
  waiting for transfers between devices  297 us (45%)
  matrix products  15.5 us (2%)
  between operations  15 us (2%)
  other arithmetic  14 us (2%)
  local copies, waits for them, and re-layouts  7.5 us (1%)
    reduce_scatter x4, waiting for transfers between devices, apply_tile(): lax.psum_scatter(direct_part, 'col', scatter_dimension=1, tiled=True)  231 us
    psum x4, blocking collectives, gram_factor(): gram = lax.psum(local_gram, ('row', 'col'))  161 us
    all_gather x4, blocking collectives, shards(): row_vectors = lax.all_gather(current, 'col', axis=1, tiled=True)  124 us
    reduce_scatter x4, waiting for transfers between devices, apply_tile(): lax.psum_scatter(transposed_part, 'row', scatter_dimension=1, tiled=True)  65.6 us
    all_gather x4, blocking collectives, shards(): col_vectors = lax.all_gather(current, 'row', axis=1, tiled=True)  21.9 us
  transfers between devices with their start and end apart: 8, of which 8 were waited for; matrix products, arithmetic and copies ran while one was open for 1% of the time, Pallas kernels for 0%

commit v1 on v0

v1 whole, which is shorter than its diff:
```python
import functools

import jax
import jax.numpy as jnp
from jax import lax
from jax.experimental import pallas as pl
from jax.experimental.pallas import tpu as pltpu
from jax.sharding import PartitionSpec as P

ITERS = 4
HIGH = lax.Precision.HIGHEST
NT = (((1,), (1,)), ((), ()))
NN = (((1,), (0,)), ((), ()))


def dot(a, b, dims):
    return lax.dot_general(a, b, dims, precision=HIGH, preferred_element_type=jnp.float32)


def factorize(gram, values):
    size = gram.shape[0]
    lanes = gram.shape[1]
    rows = lax.broadcasted_iota(jnp.int32, (size, 1), 0)
    row_grid = lax.broadcasted_iota(jnp.int32, (size, lanes), 0)
    lane_grid = lax.broadcasted_iota(jnp.int32, (size, lanes), 1)
    lower = jnp.zeros((size, lanes), jnp.float32)
    scale = jnp.zeros((size, 1), jnp.float32)
    values = list(values)
    for j in range(size):
        column = gram[:, j : j + 1]
        pivot = gram[j : j + 1, j : j + 1]
        root = 1.0 / jnp.sqrt(pivot)
        lower = jnp.where((lane_grid == j) & (row_grid >= j), column * root, lower)
        scale = jnp.where(rows == j, root, scale)
        factor = jnp.where(rows > j, column / pivot, 0.0)
        gram = gram - factor * gram[j : j + 1, :]
        values = [v - factor * v[j : j + 1, :] for v in values]
    return lower, [v * scale for v in values]


def images_of(own_ref, other_ref, slots, normalize):
    images = [own_ref[s] + other_ref[s] for s in range(slots)]
    if normalize:
        _, images = factorize(own_ref[slots] + other_ref[slots], images)
    return images


def direct_kernel(slots, normalize, meta_ref, own_ref, other_ref, tile_ref, send_ref, held_ref):
    nvec = send_ref.shape[1] // 2
    count = tile_ref.shape[0]
    for s, image in enumerate(images_of(own_ref, other_ref, slots, normalize)):
        held_ref[s] = image
    mine = held_ref[meta_ref[2 * count + 1]]
    parts = []
    for b in range(count):
        picked = held_ref[meta_ref[count + b]]
        picked = jnp.where(b < meta_ref[2 * count], picked, 0.0)
        parts.append(dot(picked, tile_ref[b], NT))
    for q in range(send_ref.shape[0]):
        send_ref[q, :nvec] = mine
        send_ref[q, nvec:] = jnp.zeros_like(mine)
    for b in range(count):
        send_ref[meta_ref[b], nvec:] += parts[b]


def transposed_kernel(slots, meta_ref, recv_ref, tile_ref, diag_ref, part_ref):
    cols, double, width = recv_ref.shape
    nvec = double // 2
    count = tile_ref.shape[0]
    parts = []
    for b in range(count):
        picked = recv_ref[meta_ref[b], :nvec]
        picked = jnp.where(b < meta_ref[2 * count], picked, 0.0)
        parts.append(dot(picked, tile_ref[b], NN))
    gram = None
    total = diag_ref[...] * recv_ref[meta_ref[2 * count + 2], :nvec]
    for c in range(cols):
        total = total + recv_ref[c, nvec:]
        piece = recv_ref[c, :nvec]
        term = dot(piece, piece, NT)
        gram = term if gram is None else gram + term
    part_ref[...] = jnp.zeros_like(part_ref)
    part_ref[slots, :, :nvec] = gram
    part_ref[meta_ref[2 * count + 1]] = total
    for b in range(count):
        part_ref[meta_ref[count + b]] += parts[b]


def last_images_kernel(slots, meta_ref, own_ref, other_ref, image_ref, send_ref, held_ref):
    nvec = send_ref.shape[1]
    gram = None
    for s, image in enumerate(images_of(own_ref, other_ref, slots, True)):
        held_ref[s] = image
        term = dot(image, image, NT)
        gram = term if gram is None else gram + term
    image_ref[...] = held_ref[meta_ref[meta_ref.shape[0] - 2]]
    gram = jnp.concatenate([gram, jnp.zeros((nvec, send_ref.shape[2] - nvec), jnp.float32)], axis=1)
    for q in range(send_ref.shape[0]):
        send_ref[q] = gram


def last_factor_kernel(image_ref, recv_ref, vector_ref, lower_ref):
    nvec = image_ref.shape[0]
    gram = recv_ref[0]
    for c in range(1, recv_ref.shape[0]):
        gram = gram + recv_ref[c]
    lower, values = factorize(gram, [image_ref[...]])
    vector_ref[...] = values[0]
    lower_ref[...] = lower[:, :nvec]


VMEM = pl.BlockSpec(memory_space=pltpu.VMEM)
SMEM = pl.BlockSpec(memory_space=pltpu.SMEM)


def shards(n_row, n_col, vectors, diagonal, blocks, block_rows, block_cols, counts):
    tile = blocks[0, 0]
    nvec, width = vectors.shape
    f32 = jnp.float32
    row, col = lax.axis_index("row"), lax.axis_index("col")
    meta = jnp.concatenate(
        [
            block_rows[0, 0],
            block_cols[0, 0],
            counts[0],
            jnp.stack([row, col]).astype(jnp.int32),
        ]
    )
    diag = diagonal[None, :]
    held = pltpu.VMEM((n_row, nvec, width), f32)
    pack = jax.ShapeDtypeStruct((n_row + 1, nvec, width), f32)
    wide = jax.ShapeDtypeStruct((n_col, 2 * nvec, width), f32)
    thin = jax.ShapeDtypeStruct((n_col, nvec, width), f32)
    piece = jax.ShapeDtypeStruct((nvec, width), f32)

    def exchange(value, step):
        return lax.ppermute(value, "row", [(i, i ^ step) for i in range(n_row)])

    def over_row(part):
        step = 1
        while 2 * step < n_row:
            part = part + exchange(part, step)
            step *= 2
        return part, exchange(part, step)

    slot = jnp.arange(n_row + 1)[:, None, None]
    part = jnp.where(slot == row, vectors[None], 0.0)
    for step in range(ITERS):
        own, other = over_row(part)
        send = pl.pallas_call(
            functools.partial(direct_kernel, n_row, step > 0),
            out_shape=wide,
            in_specs=[SMEM, VMEM, VMEM, VMEM],
            out_specs=VMEM,
            scratch_shapes=[held],
            name="direct",
        )(meta, own, other, tile)
        recv = lax.all_to_all(send, "col", 0, 0, tiled=True)
        part = pl.pallas_call(
            functools.partial(transposed_kernel, n_row),
            out_shape=pack,
            in_specs=[SMEM, VMEM, VMEM, VMEM],
            out_specs=VMEM,
            name="transposed",
        )(meta, recv, tile, diag)
    own, other = over_row(part)
    image, send = pl.pallas_call(
        functools.partial(last_images_kernel, n_row),
        out_shape=(piece, thin),
        in_specs=[SMEM, VMEM, VMEM],
        out_specs=(VMEM, VMEM),
        scratch_shapes=[held],
        name="last_images",
    )(meta, own, other)
    recv = lax.all_to_all(send, "col", 0, 0, tiled=True)
    return pl.pallas_call(
        last_factor_kernel,
        out_shape=(piece, jax.ShapeDtypeStruct((nvec, nvec), f32)),
        in_specs=[VMEM, VMEM],
        out_specs=(VMEM, VMEM),
        name="last_factor",
    )(image, recv)


def solution(mesh):
    n_row, n_col = mesh.shape["row"], mesh.shape["col"]
    if n_row & (n_row - 1) or n_row < 2:
        raise ValueError("uneven row")
    placed = (
        P(None, ("row", "col")),
        P(("row", "col")),
        P("row", "col", None, None, None),
        P("row", "col", None),
        P("row", "col", None),
        P("row", "col"),
    )
    return jax.shard_map(
        functools.partial(shards, n_row, n_col),
        mesh=mesh,
        in_specs=placed,
        out_specs=(P(None, ("row", "col")), P()),
        check_vma=False,
    )
```

time: 657 us -> 118 us (0.18)
  waiting for transfers between devices: 297 us -> 15.6 us
  blocking collectives: 307 us -> 56.3 us
  Pallas kernels: 0 us -> 26.1 us
  matrix products: 15.5 us -> 0 us
  between operations: 15 us -> 1.35 us
  other arithmetic: 14 us -> 3.08 us
  starting transfers between devices: 0.33 us -> 9.38 us
    reduce_scatter x8 -> x0, waiting for transfers between devices: 297 us -> none  [the longest x4 231 us: apply_tile(): lax.psum_scatter(direct_part, 'col', scatter_dimension=1, tiled=True)]
    psum x4 -> x0, blocking collectives: 161 us -> none  [gram_factor(): gram = lax.psum(local_gram, ('row', 'col'))]
    all_gather x8 -> x0, blocking collectives: 146 us -> none  [the longest x4 124 us: shards(): row_vectors = lax.all_gather(current, 'col', axis=1, tiled=True)]
    all_to_all x0 -> x5, blocking collectives: none -> 56.3 us  [shards(): recv = lax.all_to_all(send, 'col', 0, 0, tiled=True)]
    pallas_call x0 -> x10, Pallas kernels: none -> 26.1 us  [the longest x4 12.4 us: shards(): pl.pallas_call(functools.partial(direct_kernel, n_row, step > 0), out_sha...]
    ppermute x0 -> x10, waiting for transfers between devices: none -> 15.6 us  [exchange(): return lax.ppermute(value, 'row', [(i, i ^ step) for i in range(n_row)])]
    dot_general x28 -> x0, matrix products: 14.2 us -> none  [the longest x4 3.68 us: apply_tile(): direct = jnp.einsum('bij,kbj->kbi', tile, col_input, precision=high)]
    another operation x20 -> x0, other arithmetic: 11.3 us -> none  [the longest x8 5.68 us: solve_lower(): lax.linalg.triangular_solve(lower, values, left_side=True, lower=True)]
  transfers between devices with their start and end apart: 8 -> 10, of which waited for: 8 -> 9; matrix products, arithmetic and copies ran while one was open for 1% -> 1% of each run, Pallas kernels for 0% -> 0%
where the time goes in v1:
time: 118 us; the launch traced here: 117 us
  blocking collectives  56.3 us (48%)
  Pallas kernels  26.1 us (22%)
  waiting for transfers between devices  15.6 us (13%)
  starting transfers between devices  9.38 us (8%)
  local copies, waits for them, and re-layouts  5 us (4%)
  other arithmetic  3.08 us (3%)
  between operations  1.35 us (1%)
    all_to_all x5, blocking collectives, shards(): recv = lax.all_to_all(send, 'col', 0, 0, tiled=True)  56.3 us
    ppermute x10, waiting for transfers between devices, exchange(): return lax.ppermute(value, 'row', [(i, i ^ step) for i in range(n_row)])  15.6 us
    pallas_call x4, Pallas kernels, shards(): pl.pallas_call(functools.partial(direct_kernel, n_row, step > 0), out_sha...  12.4 us
    pallas_call x4, Pallas kernels, shards(): pl.pallas_call(functools.partial(transposed_kernel, n_row), out_shape=pac...  9.56 us
    ppermute x10, starting transfers between devices, exchange(): return lax.ppermute(value, 'row', [(i, i ^ step) for i in range(n_row)])  9.38 us
    unnamed x26, local copies, waits for them, and re-layouts  4.32 us
    add x5, other arithmetic, over_row(): part = part + exchange(part, step)  3 us
  transfers between devices with their start and end apart: 10, of which 9 were waited for; matrix products, arithmetic and copies ran while one was open for 1% of the time, Pallas kernels for 0%

profile of v1, /device:TPU:0, one launch (start us, length us, event | category | flops | bytes accessed | tf_op | source)
XLA Modules:
  0.0 116.8 jit_solution(15976773008149902511)
XLA Ops:
  2.8 2.9 %collective-permute-start.1 = (f32[5,8,128]{2,1,0:T(8,128)S(1)}, f32[5,8,128]{2,1,0:T(8,128)S(1)}, u32[]{:S(2)}, u32[]{:S(2)}) collective-permute-start(f32[5,8,128]{2,1,0:T(8,128)S(1)} %fusion.own_ref), channel_id=1, source_target_pairs={{0,16},{8,24},{16,0},{24,8},{1,17},{9,25},{17,1},{25,9},{2,18},{10... | collective-permute-start | bytes 61448 | tf_op jit(solution)/shard_map/ppermute | solution.py:137
  8.3 2.6 %direct.4 = f32[8,16,128]{2,1,0:T(8,128)} custom-call(s32[19]{0:T(128)} %concatenate.3.meta_ref, f32[5,8,128]{2,1,0:T(8,128)} %copy-done, f32[5,8,128]{2,1,0:T(8,128)} %copy-done.5, f32[8,128,128]{2,1,0:T(8,128)} %bitcast.8), custom_call_target="tpu_custom_call" | custom-call | tf_op jit(solution)/shard_map/direct/pallas_call | solution.py:150
  10.9 13.1 %all_to_all.25.recv_ref = f32[8,16,128]{2,1,0:T(8,128)} all-to-all(f32[8,16,128]{2,1,0:T(8,128)} %direct.4), channel_id=1, replica_groups=mesh['row'=4,'col'=8] {'col'}, dimensions={0} | all-to-all | bytes 131072 | tf_op jit(solution)/shard_map/all_to_all | solution.py:158
  24.0 2.4 %transposed.4 = f32[5,8,128]{2,1,0:T(8,128)} custom-call(s32[19]{0:T(128)} %concatenate.3.meta_ref, f32[8,16,128]{2,1,0:T(8,128)} %all_to_all.25.recv_ref, f32[8,128,128]{2,1,0:T(8,128)} %bitcast.9, f32[1,128]{1,0:T(1,128)} %bitcast.16), custom_call_target="tpu_custom_call" | custom-call | tf_op jit(solution)/shard_map/transposed/pallas_call | solution.py:159
  28.6 1.5 %collective-permute-start.3 = (f32[5,8,128]{2,1,0:T(8,128)S(1)}, f32[5,8,128]{2,1,0:T(8,128)S(1)}, u32[]{:S(2)}, u32[]{:S(2)}) collective-permute-start(f32[5,8,128]{2,1,0:T(8,128)S(1)} %add.16.own_ref), channel_id=1, source_target_pairs={{0,16},{8,24},{16,0},{24,8},{1,17},{9,25},{17,1},{25,9},{2,18},{10... | collective-permute-start | bytes 61448 | tf_op jit(solution)/shard_map/ppermute | solution.py:137
  30.1 2.3 %collective-permute-done.3.other_ref = f32[5,8,128]{2,1,0:T(8,128)S(1)} collective-permute-done((f32[5,8,128]{2,1,0:T(8,128)S(1)}, f32[5,8,128]{2,1,0:T(8,128)S(1)}, u32[]{:S(2)}, u32[]{:S(2)}) %collective-permute-start.3) | collective-permute-done | bytes 20512 | tf_op jit(solution)/shard_map/ppermute | solution.py:137
  33.0 3.2 %direct.5 = f32[8,16,128]{2,1,0:T(8,128)} custom-call(s32[19]{0:T(128)} %concatenate.3.meta_ref, f32[5,8,128]{2,1,0:T(8,128)} %copy-done.1, f32[5,8,128]{2,1,0:T(8,128)} %copy-done.6, f32[8,128,128]{2,1,0:T(8,128)} %bitcast.10), custom_call_target="tpu_custom_call" | custom-call | tf_op jit(solution)/shard_map/direct/pallas_call | solution.py:150
  36.2 10.9 %all_to_all.26.recv_ref = f32[8,16,128]{2,1,0:T(8,128)} all-to-all(f32[8,16,128]{2,1,0:T(8,128)} %direct.5), channel_id=1, replica_groups=mesh['row'=4,'col'=8] {'col'}, dimensions={0} | all-to-all | bytes 131072 | tf_op jit(solution)/shard_map/all_to_all | solution.py:158
  47.1 2.4 %transposed.5 = f32[5,8,128]{2,1,0:T(8,128)} custom-call(s32[19]{0:T(128)} %concatenate.3.meta_ref, f32[8,16,128]{2,1,0:T(8,128)} %all_to_all.26.recv_ref, f32[8,128,128]{2,1,0:T(8,128)} %bitcast.11, f32[1,128]{1,0:T(1,128)} %bitcast.17), custom_call_target="tpu_custom_call" | custom-call | tf_op jit(solution)/shard_map/transposed/pallas_call | solution.py:159
  51.6 1.5 %collective-permute-start.5 = (f32[5,8,128]{2,1,0:T(8,128)S(1)}, f32[5,8,128]{2,1,0:T(8,128)S(1)}, u32[]{:S(2)}, u32[]{:S(2)}) collective-permute-start(f32[5,8,128]{2,1,0:T(8,128)S(1)} %add.17.own_ref), channel_id=1, source_target_pairs={{0,16},{8,24},{16,0},{24,8},{1,17},{9,25},{17,1},{25,9},{2,18},{10... | collective-permute-start | bytes 61448 | tf_op jit(solution)/shard_map/ppermute | solution.py:137
  53.1 2.3 %collective-permute-done.5.other_ref = f32[5,8,128]{2,1,0:T(8,128)S(1)} collective-permute-done((f32[5,8,128]{2,1,0:T(8,128)S(1)}, f32[5,8,128]{2,1,0:T(8,128)S(1)}, u32[]{:S(2)}, u32[]{:S(2)}) %collective-permute-start.5) | collective-permute-done | bytes 20512 | tf_op jit(solution)/shard_map/ppermute | solution.py:137
  56.0 3.2 %direct.6 = f32[8,16,128]{2,1,0:T(8,128)} custom-call(s32[19]{0:T(128)} %concatenate.3.meta_ref, f32[5,8,128]{2,1,0:T(8,128)} %copy-done.2, f32[5,8,128]{2,1,0:T(8,128)} %copy-done.7, f32[8,128,128]{2,1,0:T(8,128)} %bitcast.12), custom_call_target="tpu_custom_call" | custom-call | tf_op jit(solution)/shard_map/direct/pallas_call | solution.py:150
  59.2 10.9 %all_to_all.27.recv_ref = f32[8,16,128]{2,1,0:T(8,128)} all-to-all(f32[8,16,128]{2,1,0:T(8,128)} %direct.6), channel_id=1, replica_groups=mesh['row'=4,'col'=8] {'col'}, dimensions={0} | all-to-all | bytes 131072 | tf_op jit(solution)/shard_map/all_to_all | solution.py:158
  70.1 2.4 %transposed.6 = f32[5,8,128]{2,1,0:T(8,128)} custom-call(s32[19]{0:T(128)} %concatenate.3.meta_ref, f32[8,16,128]{2,1,0:T(8,128)} %all_to_all.27.recv_ref, f32[8,128,128]{2,1,0:T(8,128)} %bitcast.13, f32[1,128]{1,0:T(1,128)} %bitcast.18), custom_call_target="tpu_custom_call" | custom-call | tf_op jit(solution)/shard_map/transposed/pallas_call | solution.py:159
  74.6 1.5 %collective-permute-start.7 = (f32[5,8,128]{2,1,0:T(8,128)S(1)}, f32[5,8,128]{2,1,0:T(8,128)S(1)}, u32[]{:S(2)}, u32[]{:S(2)}) collective-permute-start(f32[5,8,128]{2,1,0:T(8,128)S(1)} %add.18.own_ref), channel_id=1, source_target_pairs={{0,16},{8,24},{16,0},{24,8},{1,17},{9,25},{17,1},{25,9},{2,18},{10... | collective-permute-start | bytes 61448 | tf_op jit(solution)/shard_map/ppermute | solution.py:137
  76.1 2.3 %collective-permute-done.7.other_ref = f32[5,8,128]{2,1,0:T(8,128)S(1)} collective-permute-done((f32[5,8,128]{2,1,0:T(8,128)S(1)}, f32[5,8,128]{2,1,0:T(8,128)S(1)}, u32[]{:S(2)}, u32[]{:S(2)}) %collective-permute-start.7) | collective-permute-done | bytes 20512 | tf_op jit(solution)/shard_map/ppermute | solution.py:137
  79.0 3.2 %direct.7 = f32[8,16,128]{2,1,0:T(8,128)} custom-call(s32[19]{0:T(128)} %concatenate.3.meta_ref, f32[5,8,128]{2,1,0:T(8,128)} %copy-done.3, f32[5,8,128]{2,1,0:T(8,128)} %copy-done.8, f32[8,128,128]{2,1,0:T(8,128)} %bitcast.14), custom_call_target="tpu_custom_call" | custom-call | tf_op jit(solution)/shard_map/direct/pallas_call | solution.py:150
  82.2 10.9 %all_to_all.28.recv_ref = f32[8,16,128]{2,1,0:T(8,128)} all-to-all(f32[8,16,128]{2,1,0:T(8,128)} %direct.7), channel_id=1, replica_groups=mesh['row'=4,'col'=8] {'col'}, dimensions={0} | all-to-all | bytes 131072 | tf_op jit(solution)/shard_map/all_to_all | solution.py:158
  93.1 2.4 %transposed.7 = f32[5,8,128]{2,1,0:T(8,128)} custom-call(s32[19]{0:T(128)} %concatenate.3.meta_ref, f32[8,16,128]{2,1,0:T(8,128)} %all_to_all.28.recv_ref, f32[8,128,128]{2,1,0:T(8,128)} %bitcast.15, f32[1,128]{1,0:T(1,128)} %bitcast.19), custom_call_target="tpu_custom_call" | custom-call | tf_op jit(solution)/shard_map/transposed/pallas_call | solution.py:159
  97.6 1.5 %collective-permute-start.9 = (f32[5,8,128]{2,1,0:T(8,128)S(1)}, f32[5,8,128]{2,1,0:T(8,128)S(1)}, u32[]{:S(2)}, u32[]{:S(2)}) collective-permute-start(f32[5,8,128]{2,1,0:T(8,128)S(1)} %add.19.own_ref), channel_id=1, source_target_pairs={{0,16},{8,24},{16,0},{24,8},{1,17},{9,25},{17,1},{25,9},{2,18},{10... | collective-permute-start | bytes 61448 | tf_op jit(solution)/shard_map/ppermute | solution.py:137
  99.1 2.3 %collective-permute-done.9.other_ref = f32[5,8,128]{2,1,0:T(8,128)S(1)} collective-permute-done((f32[5,8,128]{2,1,0:T(8,128)S(1)}, f32[5,8,128]{2,1,0:T(8,128)S(1)}, u32[]{:S(2)}, u32[]{:S(2)}) %collective-permute-start.9) | collective-permute-done | bytes 20512 | tf_op jit(solution)/shard_map/ppermute | solution.py:137
  102.0 2.2 %last_images.1 = (f32[8,128]{1,0:T(8,128)}, f32[8,8,128]{2,1,0:T(8,128)}) custom-call(s32[19]{0:T(128)} %concatenate.3.meta_ref, f32[5,8,128]{2,1,0:T(8,128)} %copy-done.4, f32[5,8,128]{2,1,0:T(8,128)} %copy-done.9), custom_call_target="tpu_custom_call" | custom-call | tf_op jit(solution)/shard_map/last_images/pallas_call | solution.py:167
  104.2 10.6 %all_to_all.29.recv_ref = f32[8,8,128]{2,1,0:T(8,128)} all-to-all(f32[8,8,128]{2,1,0:T(8,128)} %get-tuple-element.5), channel_id=1, replica_groups=mesh['row'=4,'col'=8] {'col'}, dimensions={0} | all-to-all | bytes 65536 | tf_op jit(solution)/shard_map/all_to_all | solution.py:175
  114.8 2.0 %last_factor.1 = (f32[8,128]{1,0:T(8,128)}, f32[8,8]{1,0:T(8,128)}) custom-call(f32[8,128]{1,0:T(8,128)} %get-tuple-element.4.image_ref, f32[8,8,128]{2,1,0:T(8,128)} %all_to_all.29.recv_ref), custom_call_target="tpu_custom_call" | custom-call | tf_op jit(solution)/shard_map/last_factor/pallas_call | solution.py:176
  (45 shorter events, 15.0 us)
Async XLA Ops:
  0.6 0.7 copy-start.10
  1.4 1.3 %collective-permute-start = (f32[5,8,128]{2,1,0:T(8,128)S(1)}, f32[5,8,128]{2,1,0:T(8,128)S(1)}, u32[]{:S(2)}, u32[]{:S(2)}) collective-permute-start(f32[5,8,128]{2,1,0:T(8,128)S(1)} %broadcast_select_fusion), channel_id=1, source_target_pairs={{0,8},{8,0},{16,24},{24,16},{1,9},{9,1},{17,25},{25,17},{2,10},{10... | collective-permute-start | bytes 61448 | tf_op jit(solution)/shard_map/ppermute | solution.py:137
  2.8 4.9 %copy-start = (f32[5,8,128]{2,1,0:T(8,128)}, f32[5,8,128]{2,1,0:T(8,128)S(1)}, u32[]{:S(2)}) copy-start(f32[5,8,128]{2,1,0:T(8,128)S(1)} %fusion.own_ref) | copy-start | bytes 61444
  2.8 4.9 %collective-permute-start.1 = (f32[5,8,128]{2,1,0:T(8,128)S(1)}, f32[5,8,128]{2,1,0:T(8,128)S(1)}, u32[]{:S(2)}, u32[]{:S(2)}) collective-permute-start(f32[5,8,128]{2,1,0:T(8,128)S(1)} %fusion.own_ref), channel_id=1, source_target_pairs={{0,16},{8,24},{16,0},{24,8},{1,17},{9,25},{17,1},{25,9},{2,18},{10... | collective-permute-start | bytes 61448 | tf_op jit(solution)/shard_map/ppermute | solution.py:137
  6.3 0.7 copy-start.11
  6.3 0.7 copy-start.12
  7.7 0.6 copy-start.5
  26.4 1.4 %collective-permute-start.2 = (f32[5,8,128]{2,1,0:T(8,128)}, f32[5,8,128]{2,1,0:T(8,128)S(1)}, u32[]{:S(2)}, u32[]{:S(2)}) collective-permute-start(f32[5,8,128]{2,1,0:T(8,128)} %transposed.4), channel_id=1, source_target_pairs={{0,8},{8,0},{16,24},{24,16},{1,9},{9,1},{17,25},{25,17},{2,10},{10... | collective-permute-start | bytes 61448 | tf_op jit(solution)/shard_map/ppermute | solution.py:137
  28.6 3.8 %copy-start.1 = (f32[5,8,128]{2,1,0:T(8,128)}, f32[5,8,128]{2,1,0:T(8,128)S(1)}, u32[]{:S(2)}) copy-start(f32[5,8,128]{2,1,0:T(8,128)S(1)} %add.16.own_ref) | copy-start | bytes 61444
  28.6 3.8 %collective-permute-start.3 = (f32[5,8,128]{2,1,0:T(8,128)S(1)}, f32[5,8,128]{2,1,0:T(8,128)S(1)}, u32[]{:S(2)}, u32[]{:S(2)}) collective-permute-start(f32[5,8,128]{2,1,0:T(8,128)S(1)} %add.16.own_ref), channel_id=1, source_target_pairs={{0,16},{8,24},{16,0},{24,8},{1,17},{9,25},{17,1},{25,9},{2,18},{10... | collective-permute-start | bytes 61448 | tf_op jit(solution)/shard_map/ppermute | solution.py:137
  32.4 0.6 copy-start.6
  49.5 1.4 %collective-permute-start.4 = (f32[5,8,128]{2,1,0:T(8,128)}, f32[5,8,128]{2,1,0:T(8,128)S(1)}, u32[]{:S(2)}, u32[]{:S(2)}) collective-permute-start(f32[5,8,128]{2,1,0:T(8,128)} %transposed.5), channel_id=1, source_target_pairs={{0,8},{8,0},{16,24},{24,16},{1,9},{9,1},{17,25},{25,17},{2,10},{10... | collective-permute-start | bytes 61448 | tf_op jit(solution)/shard_map/ppermute | solution.py:137
  51.6 3.8 %copy-start.2 = (f32[5,8,128]{2,1,0:T(8,128)}, f32[5,8,128]{2,1,0:T(8,128)S(1)}, u32[]{:S(2)}) copy-start(f32[5,8,128]{2,1,0:T(8,128)S(1)} %add.17.own_ref) | copy-start | bytes 61444
  51.6 3.8 %collective-permute-start.5 = (f32[5,8,128]{2,1,0:T(8,128)S(1)}, f32[5,8,128]{2,1,0:T(8,128)S(1)}, u32[]{:S(2)}, u32[]{:S(2)}) collective-permute-start(f32[5,8,128]{2,1,0:T(8,128)S(1)} %add.17.own_ref), channel_id=1, source_target_pairs={{0,16},{8,24},{16,0},{24,8},{1,17},{9,25},{17,1},{25,9},{2,18},{10... | collective-permute-start | bytes 61448 | tf_op jit(solution)/shard_map/ppermute | solution.py:137
  55.4 0.6 copy-start.7
  72.5 1.4 %collective-permute-start.6 = (f32[5,8,128]{2,1,0:T(8,128)}, f32[5,8,128]{2,1,0:T(8,128)S(1)}, u32[]{:S(2)}, u32[]{:S(2)}) collective-permute-start(f32[5,8,128]{2,1,0:T(8,128)} %transposed.6), channel_id=1, source_target_pairs={{0,8},{8,0},{16,24},{24,16},{1,9},{9,1},{17,25},{25,17},{2,10},{10... | collective-permute-start | bytes 61448 | tf_op jit(solution)/shard_map/ppermute | solution.py:137
  74.6 3.8 %copy-start.3 = (f32[5,8,128]{2,1,0:T(8,128)}, f32[5,8,128]{2,1,0:T(8,128)S(1)}, u32[]{:S(2)}) copy-start(f32[5,8,128]{2,1,0:T(8,128)S(1)} %add.18.own_ref) | copy-start | bytes 61444
  74.6 3.8 %collective-permute-start.7 = (f32[5,8,128]{2,1,0:T(8,128)S(1)}, f32[5,8,128]{2,1,0:T(8,128)S(1)}, u32[]{:S(2)}, u32[]{:S(2)}) collective-permute-start(f32[5,8,128]{2,1,0:T(8,128)S(1)} %add.18.own_ref), channel_id=1, source_target_pairs={{0,16},{8,24},{16,0},{24,8},{1,17},{9,25},{17,1},{25,9},{2,18},{10... | collective-permute-start | bytes 61448 | tf_op jit(solution)/shard_map/ppermute | solution.py:137
  78.4 0.6 copy-start.8
  95.5 1.4 %collective-permute-start.8 = (f32[5,8,128]{2,1,0:T(8,128)}, f32[5,8,128]{2,1,0:T(8,128)S(1)}, u32[]{:S(2)}, u32[]{:S(2)}) collective-permute-start(f32[5,8,128]{2,1,0:T(8,128)} %transposed.7), channel_id=1, source_target_pairs={{0,8},{8,0},{16,24},{24,16},{1,9},{9,1},{17,25},{25,17},{2,10},{10... | collective-permute-start | bytes 61448 | tf_op jit(solution)/shard_map/ppermute | solution.py:137
  97.6 3.8 %copy-start.4 = (f32[5,8,128]{2,1,0:T(8,128)}, f32[5,8,128]{2,1,0:T(8,128)S(1)}, u32[]{:S(2)}) copy-start(f32[5,8,128]{2,1,0:T(8,128)S(1)} %add.19.own_ref) | copy-start | bytes 61444
  97.6 3.8 %collective-permute-start.9 = (f32[5,8,128]{2,1,0:T(8,128)S(1)}, f32[5,8,128]{2,1,0:T(8,128)S(1)}, u32[]{:S(2)}, u32[]{:S(2)}) collective-permute-start(f32[5,8,128]{2,1,0:T(8,128)S(1)} %add.19.own_ref), channel_id=1, source_target_pairs={{0,16},{8,24},{16,0},{24,8},{1,17},{9,25},{17,1},{25,9},{2,18},{10... | collective-permute-start | bytes 61448 | tf_op jit(solution)/shard_map/ppermute | solution.py:137
  101.4 0.6 copy-start.9

commit v2 on v1

--- a/solution.py
+++ b/solution.py
@@ -113,6 +113,22 @@
 SMEM = pl.BlockSpec(memory_space=pltpu.SMEM)
 
 
+def call(kernel, name, outs, meta, *operands, scratch=()):
+    specs = [VMEM] * len(operands)
+    operands = [pltpu.with_memory_space_constraint(x, pltpu.VMEM) for x in operands]
+    if meta is not None:
+        specs = [SMEM, *specs]
+        operands = [pltpu.with_memory_space_constraint(meta, pltpu.SMEM), *operands]
+    return pl.pallas_call(
+        kernel,
+        out_shape=outs,
+        in_specs=specs,
+        out_specs=jax.tree.map(lambda _: VMEM, outs),
+        scratch_shapes=scratch,
+        name=name,
+    )(*operands)
+
+
 def shards(n_row, n_col, vectors, diagonal, blocks, block_rows, block_cols, counts):
     tile = blocks[0, 0]
     nvec, width = vectors.shape
@@ -128,10 +144,10 @@
     )
     diag = diagonal[None, :]
     held = pltpu.VMEM((n_row, nvec, width), f32)
-    pack = jax.ShapeDtypeStruct((n_row + 1, nvec, width), f32)
-    wide = jax.ShapeDtypeStruct((n_col, 2 * nvec, width), f32)
-    thin = jax.ShapeDtypeStruct((n_col, nvec, width), f32)
-    piece = jax.ShapeDtypeStruct((nvec, width), f32)
+    pack = pltpu.VMEM((n_row + 1, nvec, width), f32)
+    wide = pltpu.VMEM((n_col, 2 * nvec, width), f32)
+    thin = pltpu.VMEM((n_col, nvec, width), f32)
+    piece = pltpu.VMEM((nvec, width), f32)
 
     def exchange(value, step):
         return lax.ppermute(value, "row", [(i, i ^ step) for i in range(n_row)])
@@ -147,39 +163,20 @@
     part = jnp.where(slot == row, vectors[None], 0.0)
     for step in range(ITERS):
         own, other = over_row(part)
-        send = pl.pallas_call(
-            functools.partial(direct_kernel, n_row, step > 0),
-            out_shape=wide,
-            in_specs=[SMEM, VMEM, VMEM, VMEM],
-            out_specs=VMEM,
-            scratch_shapes=[held],
-            name="direct",
-        )(meta, own, other, tile)
+        kernel = functools.partial(direct_kernel, n_row, step > 0)
+        send = call(kernel, "direct", wide, meta, own, other, tile, scratch=[held])
         recv = lax.all_to_all(send, "col", 0, 0, tiled=True)
-        part = pl.pallas_call(
-            functools.partial(transposed_kernel, n_row),
-            out_shape=pack,
-            in_specs=[SMEM, VMEM, VMEM, VMEM],
-            out_specs=VMEM,
-            name="transposed",
-        )(meta, recv, tile, diag)
+        kernel = functools.partial(transposed_kernel, n_row)
+        part = call(kernel, "transposed", pack, meta, recv, tile, diag)
     own, other = over_row(part)
-    image, send = pl.pallas_call(
-        functools.partial(last_images_kernel, n_row),
-        out_shape=(piece, thin),
-        in_specs=[SMEM, VMEM, VMEM],
-        out_specs=(VMEM, VMEM),
-        scratch_shapes=[held],
-        name="last_images",
-    )(meta, own, other)
+    kernel = functools.partial(last_images_kernel, n_row)
+    image, send = call(kernel, "last_images", (piece, thin), meta, own, other, scratch=[held])
     recv = lax.all_to_all(send, "col", 0, 0, tiled=True)
-    return pl.pallas_call(
-        last_factor_kernel,
-        out_shape=(piece, jax.ShapeDtypeStruct((nvec, nvec), f32)),
-        in_specs=[VMEM, VMEM],
-        out_specs=(VMEM, VMEM),
-        name="last_factor",
-    )(image, recv)
+    outs = (
+        jax.ShapeDtypeStruct((nvec, width), f32),
+        jax.ShapeDtypeStruct((nvec, nvec), f32),
+    )
+    return call(last_factor_kernel, "last_factor", outs, None, image, recv)
 
 
 def solution(mesh):

time: 118 us -> 96.4 us (0.82)
  Pallas kernels: 26.1 us -> 16.5 us
  blocking collectives: 56.3 us -> 50 us
  other arithmetic: 3.08 us -> 0.17 us
  local copies, waits for them, and re-layouts: 5 us -> 3.59 us
    pallas_call x10, Pallas kernels: 26.1 us -> 16.5 us  [call(): pl.pallas_call(kernel, out_shape=outs, in_specs=specs, out_specs=jax.tree...]
    all_to_all x5, blocking collectives: 56.3 us -> 50 us  [shards(): recv = lax.all_to_all(send, 'col', 0, 0, tiled=True)]
    add x5, other arithmetic: 3 us -> 0.09 us  [over_row(): part = part + exchange(part, step)]
    unnamed x26 -> x12, local copies, waits for them, and re-layouts: 4.32 us -> 3.02 us
where the time goes in v2:
time: 96.4 us; the launch traced here: 95.9 us
  blocking collectives  50 us (52%)
  Pallas kernels  16.5 us (17%)
  waiting for transfers between devices  14.7 us (15%)
  starting transfers between devices  9.62 us (10%)
  local copies, waits for them, and re-layouts  3.59 us (4%)
  between operations  1.4 us (1%)
    all_to_all x5, blocking collectives, shards(): recv = lax.all_to_all(send, 'col', 0, 0, tiled=True)  50 us
    pallas_call x10, Pallas kernels, call(): pl.pallas_call(kernel, out_shape=outs, in_specs=specs, out_specs=jax.tree...  16.5 us
    ppermute x10, waiting for transfers between devices, exchange(): return lax.ppermute(value, 'row', [(i, i ^ step) for i in range(n_row)])  14.7 us
    ppermute x10, starting transfers between devices, exchange(): return lax.ppermute(value, 'row', [(i, i ^ step) for i in range(n_row)])  9.62 us
    unnamed x12, local copies, waits for them, and re-layouts  3.02 us
  transfers between devices with their start and end apart: 10, of which 9 were waited for; matrix products, arithmetic and copies ran while one was open for 1% of the time, Pallas kernels for 0%

profile of v2, /device:TPU:0, one launch (start us, length us, event | category | flops | bytes accessed | tf_op | source)
XLA Modules:
  0.0 95.9 jit_solution(5146229171149699910)
XLA Ops:
  2.8 2.8 %collective-permute-start.1 = (f32[5,8,128]{2,1,0:T(8,128)S(1)}, f32[5,8,128]{2,1,0:T(8,128)S(1)}, u32[]{:S(2)}, u32[]{:S(2)}) collective-permute-start(f32[5,8,128]{2,1,0:T(8,128)S(1)} %fusion.own_ref), channel_id=1, source_target_pairs={{0,16},{8,24},{16,0},{24,8},{1,17},{9,25},{17,1},{25,9},{2,18},{10... | collective-permute-start | bytes 61448 | tf_op jit(solution)/shard_map/ppermute | solution.py:153
  8.6 1.7 %direct.4 = f32[8,16,128]{2,1,0:T(8,128)S(1)} custom-call(s32[19]{0:T(128)} %concatenate.3.meta_ref, f32[5,8,128]{2,1,0:T(8,128)S(1)} %fusion.own_ref, f32[5,8,128]{2,1,0:T(8,128)S(1)} %collective-permute-done.1.other_ref, f32[8,128,128]{2,1,0:T(8,128)S(1)} %bitcast.8), custom_call_target="tpu_custom_call" | custom-call | tf_op jit(solution)/shard_map/direct/pallas_call | solution.py:122
  10.3 12.9 %all_to_all.25.recv_ref = f32[8,16,128]{2,1,0:T(8,128)S(1)} all-to-all(f32[8,16,128]{2,1,0:T(8,128)S(1)} %direct.4), channel_id=1, replica_groups=mesh['row'=4,'col'=8] {'col'}, dimensions={0} | all-to-all | bytes 131072 | tf_op jit(solution)/shard_map/all_to_all | solution.py:168
  23.9 1.4 %transposed.4 = f32[5,8,128]{2,1,0:T(8,128)S(1)} custom-call(s32[19]{0:T(128)} %concatenate.3.meta_ref, f32[8,16,128]{2,1,0:T(8,128)S(1)} %all_to_all.25.recv_ref, f32[8,128,128]{2,1,0:T(8,128)S(1)} %bitcast.9, f32[1,128]{1,0:T(1,128)S(1)} %bitcast.16), custom_call_target="tpu_custom_call" | custom-call | tf_op jit(solution)/shard_map/transposed/pallas_call | solution.py:122
  26.5 1.5 %collective-permute-start.3 = (f32[5,8,128]{2,1,0:T(8,128)S(1)}, f32[5,8,128]{2,1,0:T(8,128)S(1)}, u32[]{:S(2)}, u32[]{:S(2)}) collective-permute-start(f32[5,8,128]{2,1,0:T(8,128)S(1)} %add.16.own_ref), channel_id=1, source_target_pairs={{0,16},{8,24},{16,0},{24,8},{1,17},{9,25},{17,1},{25,9},{2,18},{10... | collective-permute-start | bytes 61448 | tf_op jit(solution)/shard_map/ppermute | solution.py:153
  28.0 2.3 %collective-permute-done.3.other_ref = f32[5,8,128]{2,1,0:T(8,128)S(1)} collective-permute-done((f32[5,8,128]{2,1,0:T(8,128)S(1)}, f32[5,8,128]{2,1,0:T(8,128)S(1)}, u32[]{:S(2)}, u32[]{:S(2)}) %collective-permute-start.3) | collective-permute-done | bytes 20512 | tf_op jit(solution)/shard_map/ppermute | solution.py:153
  30.3 2.2 %direct.5 = f32[8,16,128]{2,1,0:T(8,128)S(1)} custom-call(s32[19]{0:T(128)} %concatenate.3.meta_ref, f32[5,8,128]{2,1,0:T(8,128)S(1)} %add.16.own_ref, f32[5,8,128]{2,1,0:T(8,128)S(1)} %collective-permute-done.3.other_ref, f32[8,128,128]{2,1,0:T(8,128)S(1)} %bitcast.10), custom_call_target="tpu_custom_call" | custom-call | tf_op jit(solution)/shard_map/direct/pallas_call | solution.py:122
  32.5 9.3 %all_to_all.26.recv_ref = f32[8,16,128]{2,1,0:T(8,128)S(1)} all-to-all(f32[8,16,128]{2,1,0:T(8,128)S(1)} %direct.5), channel_id=1, replica_groups=mesh['row'=4,'col'=8] {'col'}, dimensions={0} | all-to-all | bytes 131072 | tf_op jit(solution)/shard_map/all_to_all | solution.py:168
  41.8 1.4 %transposed.5 = f32[5,8,128]{2,1,0:T(8,128)S(1)} custom-call(s32[19]{0:T(128)} %concatenate.3.meta_ref, f32[8,16,128]{2,1,0:T(8,128)S(1)} %all_to_all.26.recv_ref, f32[8,128,128]{2,1,0:T(8,128)S(1)} %bitcast.11, f32[1,128]{1,0:T(1,128)S(1)} %bitcast.17), custom_call_target="tpu_custom_call" | custom-call | tf_op jit(solution)/shard_map/transposed/pallas_call | solution.py:122
  44.5 1.5 %collective-permute-start.5 = (f32[5,8,128]{2,1,0:T(8,128)S(1)}, f32[5,8,128]{2,1,0:T(8,128)S(1)}, u32[]{:S(2)}, u32[]{:S(2)}) collective-permute-start(f32[5,8,128]{2,1,0:T(8,128)S(1)} %add.17.own_ref), channel_id=1, source_target_pairs={{0,16},{8,24},{16,0},{24,8},{1,17},{9,25},{17,1},{25,9},{2,18},{10... | collective-permute-start | bytes 61448 | tf_op jit(solution)/shard_map/ppermute | solution.py:153
  46.0 2.3 %collective-permute-done.5.other_ref = f32[5,8,128]{2,1,0:T(8,128)S(1)} collective-permute-done((f32[5,8,128]{2,1,0:T(8,128)S(1)}, f32[5,8,128]{2,1,0:T(8,128)S(1)}, u32[]{:S(2)}, u32[]{:S(2)}) %collective-permute-start.5) | collective-permute-done | bytes 20512 | tf_op jit(solution)/shard_map/ppermute | solution.py:153
  48.3 2.2 %direct.6 = f32[8,16,128]{2,1,0:T(8,128)S(1)} custom-call(s32[19]{0:T(128)} %concatenate.3.meta_ref, f32[5,8,128]{2,1,0:T(8,128)S(1)} %add.17.own_ref, f32[5,8,128]{2,1,0:T(8,128)S(1)} %collective-permute-done.5.other_ref, f32[8,128,128]{2,1,0:T(8,128)S(1)} %bitcast.12), custom_call_target="tpu_custom_call" | custom-call | tf_op jit(solution)/shard_map/direct/pallas_call | solution.py:122
  50.4 9.3 %all_to_all.27.recv_ref = f32[8,16,128]{2,1,0:T(8,128)S(1)} all-to-all(f32[8,16,128]{2,1,0:T(8,128)S(1)} %direct.6), channel_id=1, replica_groups=mesh['row'=4,'col'=8] {'col'}, dimensions={0} | all-to-all | bytes 131072 | tf_op jit(solution)/shard_map/all_to_all | solution.py:168
  59.7 1.4 %transposed.6 = f32[5,8,128]{2,1,0:T(8,128)S(1)} custom-call(s32[19]{0:T(128)} %concatenate.3.meta_ref, f32[8,16,128]{2,1,0:T(8,128)S(1)} %all_to_all.27.recv_ref, f32[8,128,128]{2,1,0:T(8,128)S(1)} %bitcast.13, f32[1,128]{1,0:T(1,128)S(1)} %bitcast.18), custom_call_target="tpu_custom_call" | custom-call | tf_op jit(solution)/shard_map/transposed/pallas_call | solution.py:122
  62.4 1.5 %collective-permute-start.7 = (f32[5,8,128]{2,1,0:T(8,128)S(1)}, f32[5,8,128]{2,1,0:T(8,128)S(1)}, u32[]{:S(2)}, u32[]{:S(2)}) collective-permute-start(f32[5,8,128]{2,1,0:T(8,128)S(1)} %add.18.own_ref), channel_id=1, source_target_pairs={{0,16},{8,24},{16,0},{24,8},{1,17},{9,25},{17,1},{25,9},{2,18},{10... | collective-permute-start | bytes 61448 | tf_op jit(solution)/shard_map/ppermute | solution.py:153
  63.9 2.3 %collective-permute-done.7.other_ref = f32[5,8,128]{2,1,0:T(8,128)S(1)} collective-permute-done((f32[5,8,128]{2,1,0:T(8,128)S(1)}, f32[5,8,128]{2,1,0:T(8,128)S(1)}, u32[]{:S(2)}, u32[]{:S(2)}) %collective-permute-start.7) | collective-permute-done | bytes 20512 | tf_op jit(solution)/shard_map/ppermute | solution.py:153
  66.2 2.2 %direct.7 = f32[8,16,128]{2,1,0:T(8,128)S(1)} custom-call(s32[19]{0:T(128)} %concatenate.3.meta_ref, f32[5,8,128]{2,1,0:T(8,128)S(1)} %add.18.own_ref, f32[5,8,128]{2,1,0:T(8,128)S(1)} %collective-permute-done.7.other_ref, f32[8,128,128]{2,1,0:T(8,128)S(1)} %bitcast.14), custom_call_target="tpu_custom_call" | custom-call | tf_op jit(solution)/shard_map/direct/pallas_call | solution.py:122
  68.3 9.3 %all_to_all.28.recv_ref = f32[8,16,128]{2,1,0:T(8,128)S(1)} all-to-all(f32[8,16,128]{2,1,0:T(8,128)S(1)} %direct.7), channel_id=1, replica_groups=mesh['row'=4,'col'=8] {'col'}, dimensions={0} | all-to-all | bytes 131072 | tf_op jit(solution)/shard_map/all_to_all | solution.py:168
  77.7 1.4 %transposed.7 = f32[5,8,128]{2,1,0:T(8,128)S(1)} custom-call(s32[19]{0:T(128)} %concatenate.3.meta_ref, f32[8,16,128]{2,1,0:T(8,128)S(1)} %all_to_all.28.recv_ref, f32[8,128,128]{2,1,0:T(8,128)S(1)} %bitcast.15, f32[1,128]{1,0:T(1,128)S(1)} %bitcast.19), custom_call_target="tpu_custom_call" | custom-call | tf_op jit(solution)/shard_map/transposed/pallas_call | solution.py:122
  80.3 1.5 %collective-permute-start.9 = (f32[5,8,128]{2,1,0:T(8,128)S(1)}, f32[5,8,128]{2,1,0:T(8,128)S(1)}, u32[]{:S(2)}, u32[]{:S(2)}) collective-permute-start(f32[5,8,128]{2,1,0:T(8,128)S(1)} %add.19.own_ref), channel_id=1, source_target_pairs={{0,16},{8,24},{16,0},{24,8},{1,17},{9,25},{17,1},{25,9},{2,18},{10... | collective-permute-start | bytes 61448 | tf_op jit(solution)/shard_map/ppermute | solution.py:153
  81.8 2.3 %collective-permute-done.9.other_ref = f32[5,8,128]{2,1,0:T(8,128)S(1)} collective-permute-done((f32[5,8,128]{2,1,0:T(8,128)S(1)}, f32[5,8,128]{2,1,0:T(8,128)S(1)}, u32[]{:S(2)}, u32[]{:S(2)}) %collective-permute-start.9) | collective-permute-done | bytes 20512 | tf_op jit(solution)/shard_map/ppermute | solution.py:153
  84.1 1.5 %last_images.1 = (f32[8,128]{1,0:T(8,128)S(1)}, f32[8,8,128]{2,1,0:T(8,128)S(1)}) custom-call(s32[19]{0:T(128)} %concatenate.3.meta_ref, f32[5,8,128]{2,1,0:T(8,128)S(1)} %add.19.own_ref, f32[5,8,128]{2,1,0:T(8,128)S(1)} %collective-permute-done.9.other_ref), custom_call_target="tpu_custom_call" | custom-call | tf_op jit(solution)/shard_map/last_images/pallas_call | solution.py:122
  85.6 9.1 %all_to_all.29.recv_ref = f32[8,8,128]{2,1,0:T(8,128)S(1)} all-to-all(f32[8,8,128]{2,1,0:T(8,128)S(1)} %get-tuple-element.5), channel_id=1, replica_groups=mesh['row'=4,'col'=8] {'col'}, dimensions={0} | all-to-all | bytes 65536 | tf_op jit(solution)/shard_map/all_to_all | solution.py:174
  94.6 1.2 %last_factor.1 = (f32[8,128]{1,0:T(8,128)}, f32[8,8]{1,0:T(8,128)}) custom-call(f32[8,128]{1,0:T(8,128)S(1)} %get-tuple-element.4.image_ref, f32[8,8,128]{2,1,0:T(8,128)S(1)} %all_to_all.29.recv_ref), custom_call_target="tpu_custom_call" | custom-call | tf_op jit(solution)/shard_map/last_factor/pallas_call | solution.py:122
  (31 shorter events, 10.1 us)
Async XLA Ops:
  0.6 0.7 copy-start.3
  1.4 1.3 %collective-permute-start = (f32[5,8,128]{2,1,0:T(8,128)S(1)}, f32[5,8,128]{2,1,0:T(8,128)S(1)}, u32[]{:S(2)}, u32[]{:S(2)}) collective-permute-start(f32[5,8,128]{2,1,0:T(8,128)S(1)} %broadcast_select_fusion), channel_id=1, source_target_pairs={{0,8},{8,0},{16,24},{24,16},{1,9},{9,1},{17,25},{25,17},{2,10},{10... | collective-permute-start | bytes 61448 | tf_op jit(solution)/shard_map/ppermute | solution.py:153
  2.8 4.7 %collective-permute-start.1 = (f32[5,8,128]{2,1,0:T(8,128)S(1)}, f32[5,8,128]{2,1,0:T(8,128)S(1)}, u32[]{:S(2)}, u32[]{:S(2)}) collective-permute-start(f32[5,8,128]{2,1,0:T(8,128)S(1)} %fusion.own_ref), channel_id=1, source_target_pairs={{0,16},{8,24},{16,0},{24,8},{1,17},{9,25},{17,1},{25,9},{2,18},{10... | collective-permute-start | bytes 61448 | tf_op jit(solution)/shard_map/ppermute | solution.py:153
  6.3 0.7 copy-start.4
  6.3 0.7 copy-start.5
  7.5 1.0 %copy-start = (f32[1,1,8,128,128]{4,3,2,1,0:T(8,128)S(1)}, f32[1,1,8,128,128]{4,3,2,1,0:T(8,128)}, u32[]{:S(2)}) copy-start(f32[1,1,8,128,128]{4,3,2,1,0:T(8,128)} %param.8) | copy-start | bytes 1572868
  8.6 14.7 %copy-start.1 = (f32[1,1,8,128,128]{4,3,2,1,0:T(8,128)S(1)}, f32[1,1,8,128,128]{4,3,2,1,0:T(8,128)}, u32[]{:S(2)}) copy-start(f32[1,1,8,128,128]{4,3,2,1,0:T(8,128)} %param.8) | copy-start | bytes 1572868
  23.2 0.7 copy-start.2
  25.3 1.3 %collective-permute-start.2 = (f32[5,8,128]{2,1,0:T(8,128)S(1)}, f32[5,8,128]{2,1,0:T(8,128)S(1)}, u32[]{:S(2)}, u32[]{:S(2)}) collective-permute-start(f32[5,8,128]{2,1,0:T(8,128)S(1)} %transposed.4), channel_id=1, source_target_pairs={{0,8},{8,0},{16,24},{24,16},{1,9},{9,1},{17,25},{25,17},{2,10},{10... | collective-permute-start | bytes 61448 | tf_op jit(solution)/shard_map/ppermute | solution.py:153
  26.5 3.8 %collective-permute-start.3 = (f32[5,8,128]{2,1,0:T(8,128)S(1)}, f32[5,8,128]{2,1,0:T(8,128)S(1)}, u32[]{:S(2)}, u32[]{:S(2)}) collective-permute-start(f32[5,8,128]{2,1,0:T(8,128)S(1)} %add.16.own_ref), channel_id=1, source_target_pairs={{0,16},{8,24},{16,0},{24,8},{1,17},{9,25},{17,1},{25,9},{2,18},{10... | collective-permute-start | bytes 61448 | tf_op jit(solution)/shard_map/ppermute | solution.py:153
  43.2 1.3 %collective-permute-start.4 = (f32[5,8,128]{2,1,0:T(8,128)S(1)}, f32[5,8,128]{2,1,0:T(8,128)S(1)}, u32[]{:S(2)}, u32[]{:S(2)}) collective-permute-start(f32[5,8,128]{2,1,0:T(8,128)S(1)} %transposed.5), channel_id=1, source_target_pairs={{0,8},{8,0},{16,24},{24,16},{1,9},{9,1},{17,25},{25,17},{2,10},{10... | collective-permute-start | bytes 61448 | tf_op jit(solution)/shard_map/ppermute | solution.py:153
  44.5 3.8 %collective-permute-start.5 = (f32[5,8,128]{2,1,0:T(8,128)S(1)}, f32[5,8,128]{2,1,0:T(8,128)S(1)}, u32[]{:S(2)}, u32[]{:S(2)}) collective-permute-start(f32[5,8,128]{2,1,0:T(8,128)S(1)} %add.17.own_ref), channel_id=1, source_target_pairs={{0,16},{8,24},{16,0},{24,8},{1,17},{9,25},{17,1},{25,9},{2,18},{10... | collective-permute-start | bytes 61448 | tf_op jit(solution)/shard_map/ppermute | solution.py:153
  61.1 1.3 %collective-permute-start.6 = (f32[5,8,128]{2,1,0:T(8,128)S(1)}, f32[5,8,128]{2,1,0:T(8,128)S(1)}, u32[]{:S(2)}, u32[]{:S(2)}) collective-permute-start(f32[5,8,128]{2,1,0:T(8,128)S(1)} %transposed.6), channel_id=1, source_target_pairs={{0,8},{8,0},{16,24},{24,16},{1,9},{9,1},{17,25},{25,17},{2,10},{10... | collective-permute-start | bytes 61448 | tf_op jit(solution)/shard_map/ppermute | solution.py:153
  62.4 3.8 %collective-permute-start.7 = (f32[5,8,128]{2,1,0:T(8,128)S(1)}, f32[5,8,128]{2,1,0:T(8,128)S(1)}, u32[]{:S(2)}, u32[]{:S(2)}) collective-permute-start(f32[5,8,128]{2,1,0:T(8,128)S(1)} %add.18.own_ref), channel_id=1, source_target_pairs={{0,16},{8,24},{16,0},{24,8},{1,17},{9,25},{17,1},{25,9},{2,18},{10... | collective-permute-start | bytes 61448 | tf_op jit(solution)/shard_map/ppermute | solution.py:153
  79.1 1.3 %collective-permute-start.8 = (f32[5,8,128]{2,1,0:T(8,128)S(1)}, f32[5,8,128]{2,1,0:T(8,128)S(1)}, u32[]{:S(2)}, u32[]{:S(2)}) collective-permute-start(f32[5,8,128]{2,1,0:T(8,128)S(1)} %transposed.7), channel_id=1, source_target_pairs={{0,8},{8,0},{16,24},{24,16},{1,9},{9,1},{17,25},{25,17},{2,10},{10... | collective-permute-start | bytes 61448 | tf_op jit(solution)/shard_map/ppermute | solution.py:153
  80.3 3.8 %collective-permute-start.9 = (f32[5,8,128]{2,1,0:T(8,128)S(1)}, f32[5,8,128]{2,1,0:T(8,128)S(1)}, u32[]{:S(2)}, u32[]{:S(2)}) collective-permute-start(f32[5,8,128]{2,1,0:T(8,128)S(1)} %add.19.own_ref), channel_id=1, source_target_pairs={{0,16},{8,24},{16,0},{24,8},{1,17},{9,25},{17,1},{25,9},{2,18},{10... | collective-permute-start | bytes 61448 | tf_op jit(solution)/shard_map/ppermute | solution.py:153
